TPU v7x, 32 devices: a whole 2x2x4 slice. The times are simulated.
32 devices in a mesh: cfg: 2 (over x), space: 16 (over z, y, core).
Axes of the slice: x: 2, y: 2, z: 4, core: 2. Of those that a mesh axis runs over, the one named last changes fastest.
Arguments:
- eigenvectors: bfloat16 [8, 2, 3, 128, 16, 1024], P('cfg', None, None, None, 'space'), parts along dimension 0, may hold values from -3 to 3
- link_field: bfloat16 [8, 3, 2, 3, 3, 16, 1024], P('cfg', None, None, None, None, 'space'), parts along dimension 0, may hold values from -2.5 to 2.5
- momentum: int32 [3], replicated, may hold values from -2 to 2
- directions: int32 [4], replicated, may hold values from 0 to 2, as said below
- offsets: int32 [4], replicated, may hold values from 0 to 124
Outputs:
- elementals: float32 [8, 2, 4, 128, 128], P('cfg', None, None, 'space'), parts along dimension 0
There are 2 independent parts, one for each index of `cfg`. A program takes and returns all parts, laid end to end along the dimension named above; an argument that names none is the same for every part. Nothing has to cross between parts.
Inputs may be any that keep to these rules, and one draw needn't show every extreme that they name: `directions`: exactly 2 of the timeslices have direction 0 (the first dimension); each other one has direction 1 or 2.
All inputs are finite; a program needn't handle non-finite values.
Results may differ from a plain program's by a relative error of at most 0.0041.
Values may be sent and summed in bfloat16 or wider, within the bound.
No kernel may reach another device: no remote copies, remote signals or barrier semaphores. Data moves between devices by JAX's collectives and lax.ppermute only.
A program may use at most 128 MiB of HBM per device.

v0:
```python
import math

import jax
import jax.numpy as jnp
from jax import lax
from jax.experimental import pallas as pl
from jax.experimental.pallas import tpu as pltpu
from jax.sharding import PartitionSpec as P

BLK = 4
LY = 32
LZ = 32
ROWS = 16
LANES = 128

epsilon_cycles = ((0, 1, 2), (1, 2, 0), (2, 0, 1))


def phase_table(momentum, x_site, extent):
    y_sites = jnp.arange(LY, dtype=jnp.int32)
    z_sites = jnp.arange(LZ, dtype=jnp.int32)
    x_turns = (momentum[0] * x_site % extent).astype(jnp.float32) / extent
    y_turns = (momentum[1] * y_sites % LY).astype(jnp.float32) / LY
    z_turns = (momentum[2] * z_sites % LZ).astype(jnp.float32) / LZ
    angles = -2.0 * math.pi * (x_turns + y_turns[:, None] + z_turns[None, :])
    angles = angles.reshape(LY * LZ)
    return jnp.cos(angles), jnp.sin(angles)


def shift_inside(direction, vec_ref, src_ref):
    nev, sites = vec_ref.shape[-2:]

    def fill(shifted):
        def step(block, carry):
            rows = pl.ds(pl.multiple_of(block * ROWS, ROWS), ROWS)
            for part in range(2):
                for color in range(3):
                    values = vec_ref[0, part, color, rows, :].astype(jnp.float32)
                    src_ref[part, color, rows, :] = shifted(values).astype(jnp.bfloat16)
            return carry

        lax.fori_loop(0, nev // ROWS, step, 0)

    def along_third(values):
        lane = lax.broadcasted_iota(jnp.int32, values.shape, 1)
        ahead = pltpu.roll(values, sites - 1, 1)
        wrapped = pltpu.roll(values, LZ - 1, 1)
        return jnp.where(lane % LZ == LZ - 1, wrapped, ahead)

    @pl.when(direction == 1)
    def _():
        fill(lambda values: pltpu.roll(values, sites - LZ, 1))

    @pl.when(direction != 1)
    def _():
        fill(along_third)


def elementals_kernel(shifting, scale, *refs):
    if shifting:
        meta_ref, vec_ref, link_ref, lead_ref, out_ref, prod_ref, rhs_ref, u_ref, src_ref = refs
        shift_inside(meta_ref[1, pl.program_id(0)], vec_ref, src_ref)
    else:
        meta_ref, vec_ref, link_ref, lead_ref, src_ref, out_ref, prod_ref, rhs_ref, u_ref = refs
    nev, sites = vec_ref.shape[-2:]

    for entry in range(9):
        pair = link_ref[0, 0, entry].astype(jnp.float32)
        u_re, u_im = pair[0:1], pair[1:2]
        u_ref[entry : entry + 1, :] = u_re
        u_ref[9 + entry : 10 + entry, :] = u_im - u_re
        u_ref[18 + entry : 19 + entry, :] = u_re + u_im

    for color in range(3):
        vec_re = vec_ref[0, 0, color]
        vec_im = vec_ref[0, 1, color]
        first = slice(color * sites, (color + 1) * sites)
        second = slice((3 + color) * sites, (4 + color) * sites)
        rhs_ref[0:nev, first] = vec_re
        rhs_ref[nev : 2 * nev, first] = vec_im
        rhs_ref[0:nev, second] = -vec_im
        rhs_ref[nev : 2 * nev, second] = vec_re

    def lane_step(lane_block, carry):
        lane = pl.multiple_of(lane_block * LANES, LANES)
        lanes = pl.ds(lane, LANES)

        def row(ref, index):
            return jnp.broadcast_to(ref[pl.ds(index, 1), lanes], (ROWS, LANES))

        def lead_row(index):
            return jnp.broadcast_to(lead_ref[0, pl.ds(index, 1), lanes], (ROWS, LANES))

        def row_step(block, carry):
            rows = pl.ds(pl.multiple_of(block * ROWS, ROWS), ROWS)
            s_re = [src_ref[0, j, rows, lanes].astype(jnp.float32) for j in range(3)]
            s_im = [src_ref[1, j, rows, lanes].astype(jnp.float32) for j in range(3)]
            s_sum = [s_re[j] + s_im[j] for j in range(3)]
            d_re, d_im, d_sum = [], [], []
            for i in range(3):
                k1 = k2 = k3 = None
                for j in range(3):
                    entry = 3 * i + j
                    t1 = row(u_ref, entry) * s_sum[j]
                    t2 = row(u_ref, 9 + entry) * s_re[j]
                    t3 = row(u_ref, 18 + entry) * s_im[j]
                    k1 = t1 if k1 is None else k1 + t1
                    k2 = t2 if k2 is None else k2 + t2
                    k3 = t3 if k3 is None else k3 + t3
                re = (k1 - k3).astype(jnp.bfloat16).astype(jnp.float32)
                im = (k1 + k2).astype(jnp.bfloat16).astype(jnp.float32)
                d_re.append(re)
                d_im.append(im)
                d_sum.append(re + im)
            for a in range(BLK):
                out_rows = pl.ds(pl.multiple_of(block * ROWS + a * nev, ROWS), ROWS)
                for i, j, k in epsilon_cycles:
                    at_i, at_j = 3 * a + i, 3 * a + j
                    k1 = lead_row(at_i) * d_sum[j] - lead_row(at_j) * d_sum[i]
                    k2 = lead_row(12 + at_i) * d_re[j] - lead_row(12 + at_j) * d_re[i]
                    k3 = lead_row(24 + at_i) * d_im[j] - lead_row(24 + at_j) * d_im[i]
                    first = pl.ds(pl.multiple_of(lane + k * sites, LANES), LANES)
                    second = pl.ds(pl.multiple_of(lane + (3 + k) * sites, LANES), LANES)
                    prod_ref[out_rows, first] = (k1 - k3).astype(jnp.bfloat16)
                    prod_ref[out_rows, second] = (k1 + k2).astype(jnp.bfloat16)
            return carry

        return lax.fori_loop(0, nev // ROWS, row_step, carry)

    lax.fori_loop(0, sites // LANES, lane_step, 0)

    sums = lax.dot_general(
        prod_ref[...],
        rhs_ref[...],
        (((1,), (1,)), ((), ())),
        preferred_element_type=jnp.float32,
    )
    sums = sums * scale
    for part in range(2):
        for a in range(BLK):
            block = sums[a * nev : (a + 1) * nev, part * nev : (part + 1) * nev]
            out_ref[0, part * BLK + a] = block.astype(jnp.bfloat16)


def elementals_call(shifting, scale, meta, vectors, links, leads, source=None):
    count = meta.shape[1]
    _, _, _, nev, sites = vectors.shape
    in_specs = [
        pl.BlockSpec((1, 2, 3, nev, sites), lambda n, meta: (meta[0, n], 0, 0, 0, 0)),
        pl.BlockSpec((1, 1, 9, 2, sites), lambda n, meta: (meta[0, n], meta[1, n], 0, 0, 0)),
        pl.BlockSpec((1, 9 * BLK, sites), lambda n, meta: (meta[0, n], 0, 0)),
    ]
    operands = [meta, vectors, links, leads]
    scratch = [
        pltpu.VMEM((BLK * nev, 6 * sites), jnp.bfloat16),
        pltpu.VMEM((2 * nev, 6 * sites), jnp.bfloat16),
        pltpu.VMEM((32, sites), jnp.float32),
    ]
    if shifting:
        scratch.append(pltpu.VMEM((2, 3, nev, sites), jnp.bfloat16))
    else:
        in_specs.append(pl.BlockSpec((2, 3, nev, sites), lambda n, meta: (0, 0, 0, 0)))
        operands.append(source)

    def body(*refs):
        elementals_kernel(shifting, scale, *refs)

    return pl.pallas_call(
        body,
        out_shape=jax.ShapeDtypeStruct((count, 2 * BLK, nev, nev), jnp.bfloat16),
        grid_spec=pltpu.PrefetchScalarGridSpec(
            num_scalar_prefetch=1,
            grid=(count,),
            in_specs=in_specs,
            out_specs=pl.BlockSpec((1, 2 * BLK, nev, nev), lambda n, meta: (n, 0, 0, 0)),
            scratch_shapes=scratch,
        ),
        compiler_params=pltpu.CompilerParams(
            dimension_semantics=("arbitrary",), vmem_limit_bytes=48 * 1024 * 1024
        ),
        cost_estimate=pl.CostEstimate(
            flops=count * 16 * BLK * 3 * nev * nev * sites,
            bytes_accessed=count * 16 * 3 * nev * sites,
            transcendentals=0,
        ),
        name="shift_elementals" if shifting else "halo_elementals",
    )(*operands)


def on_device(eigenvectors, link_field, momentum, directions, offsets):
    devices = lax.axis_size("space")
    tsl, _, _, nev, planes, sites = eigenvectors.shape
    assert planes == 1
    extent_x = planes * devices
    scale = 1.0 / math.sqrt(extent_x * sites)
    vectors = eigenvectors.reshape(tsl, 2, 3, nev, sites)
    links = jnp.transpose(link_field, (0, 1, 3, 4, 5, 2, 6)).reshape(tsl, 3, 9, 2, sites)

    order = jnp.argsort(jnp.where(directions == 0, 1, 0), stable=True).astype(jnp.int32)
    meta = jnp.stack([order, directions[order]])
    half = tsl // 2

    pairs = [(device, (device - 1) % devices) for device in range(devices)]
    halos = [
        lax.ppermute(
            lax.dynamic_index_in_dim(vectors, order[half + n], 0, keepdims=False), "space", pairs
        )
        for n in range(half)
    ]

    cosine, sine = phase_table(momentum, lax.axis_index("space"), extent_x)
    lead = jnp.stack(
        [lax.dynamic_slice_in_dim(vectors[t], offsets[t], BLK, axis=2) for t in range(tsl)]
    ).astype(jnp.float32)
    lead = jnp.swapaxes(lead, 2, 3)
    lead_re = lead[:, 0] * cosine - lead[:, 1] * sine
    lead_im = lead[:, 0] * sine + lead[:, 1] * cosine
    leads = jnp.stack([lead_re, lead_im - lead_re, lead_re + lead_im], axis=1)
    leads = leads.reshape(tsl, 9 * BLK, sites)

    def spread(partial):
        count = partial.shape[0]
        parts = partial.reshape(count, 2 * BLK, devices, nev // devices, nev)
        parts = jnp.moveaxis(parts, 2, 0)
        parts = lax.all_to_all(parts, "space", 0, 0, tiled=True)
        return jnp.sum(parts.astype(jnp.float32), axis=0)

    partials = [elementals_call(True, scale, meta[:, :half], vectors, links, leads)]
    for n in range(half):
        where = meta[:, half + n : half + n + 1]
        partials.append(elementals_call(False, scale, where, vectors, links, leads, halos[n]))
    early = spread(jnp.concatenate(partials[:-1]))
    late = spread(partials[-1])
    sums = jnp.concatenate([early, late])
    back = jnp.argsort(order)
    sums = jnp.take(sums, back, axis=0)
    return sums.reshape(tsl, 2, BLK, nev // devices, nev)


def solution(mesh):
    placed = (
        P("cfg", None, None, None, "space", None),
        P("cfg", None, None, None, None, "space", None),
        P(),
        P(),
        P(),
    )
    return jax.shard_map(
        on_device,
        mesh=mesh,
        in_specs=placed,
        out_specs=P("cfg", None, None, "space", None),
        check_vma=False,
    )
```

profile of v0, /device:TPU:0, one launch (start us, length us, event | category | flops | bytes accessed | tf_op | source)
XLA Modules:
  0.0 126.4 jit_solution(9764021035882111709)
XLA Ops:
  0.0 0.7 compare_select_fusion.6
  0.7 0.7 sort.34
  1.4 0.7 fusion.12
  6.1 7.1 %dynamic-slice_bitcast_fusion.1 = (bf16[2,3,128,1024]{3,2,1,0:T(8,128)(2,1)}, bf16[1,2,3,128,1,1024]{5,3,4,2,1,0:T(8,128)(2,1)S(1)}, bf16[1,2,3,128,1,1024]{5,3,...) fusion(bf16[4,2,3,128,1,1024]{5,3,4,2,1,0:T(8,128)(2,1)} %param, ...), kind=kLoop, calls=%fused_computation.4 | loop fusion | bytes 18874376 | tf_op jit(solution)/shard_map/jit(dynamic_index_in_dim)/squeeze | solution.py:206
  13.2 5.5 %collective-permute-start = (bf16[2,3,128,1024]{3,2,1,0:T(8,128)(2,1)}, bf16[2,3,128,1024]{3,2,1,0:T(8,128)(2,1)S(1)}, u32[]{:S(2)}, u32[]{:S(2)}) collective-permute-start(bf16[2,3,128,1024]{3,2,1,0:T(8,128)(2,1)} %get-tuple-element.11), channel_id=1, source_target_pairs={{0,15},{1,0},{2,1},{3,2},{4,3},{5,4},{6,5},{7,6},{8,7},{9,8},{10,9... | collective-permute-start | bytes 4718600 | tf_op jit(solution)/shard_map/ppermute | solution.py:205
  18.6 0.7 collective-permute-start.1
  19.3 0.7 fusion.13
  25.2 0.6 fusion.14
  26.5 1.3 fusion.4
  30.7 1.1 dynamic-slice_bitcast_fusion.4
  31.8 1.0 dynamic-slice_bitcast_fusion.2
  34.1 0.6 gather_fusion
  34.9 18.9 %collective-permute-done.1.refs_4_ = bf16[2,3,128,1024]{3,2,1,0:T(8,128)(2,1)} collective-permute-done((bf16[2,3,128,1024]{3,2,1,0:T(8,128)(2,1)}, bf16[2,3,128,1024]{3,2,1,0:T(8,128)(2,1)}, u32[]{:S(2)}, u32[]{:S(2)}) %collective-permute-start.1) | collective-permute-done | bytes 1572896 | tf_op jit(solution)/shard_map/ppermute | solution.py:205
  53.7 9.9 %halo_elementals.3 = bf16[1,8,128,128]{3,2,1,0:T(8,128)(2,1)S(1)} custom-call(s32[2,1]{1,0:T(2,128)S(1)} %get-tuple-element.18.refs_0_, bf16[4,2,3,128,1024]{4,3,2,1,0:T(8,128)(2,1)} %bitcast.47, bf16[4,3,9,2,1024]{4,3,2,1,0:T(2,128)(2,1)S(1)} %bitcast.44, f32[4,36,1024]{2,1,0:T(8,128)S(1)} %copy.11.refs_3_, ...), custom_call_target="tpu_custom_call" | custom-call | flops 3221225472 | bytes 6291456 | tf_op jit(solution)/shard_map/halo_elementals/pallas_call | solution.py:168
  63.6 0.8 copy_bitcast_fusion.1
  64.4 6.0 %all-to-all-start.1 = ((bf16[16,1,8,8,128]{4,3,2,1,0:T(8,128)(2,1)}), bf16[16,1,8,8,128]{4,3,2,1,0:T(8,128)(2,1)S(1)}, u32[]{:S(2)}, u32[]{:S(2)}) async-start(bf16[16,1,8,8,128]{4,3,2,1,0:T(8,128)(2,1)} %copy_bitcast_fusion.1), calls=%async_computation.1 | async-start | bytes 524288 | tf_op jit(solution)/shard_map/all_to_all | solution.py:225
  70.4 19.4 %shift_elementals.1 = bf16[2,8,128,128]{3,2,1,0:T(8,128)(2,1)S(1)} custom-call(s32[2,2]{1,0:T(2,128)S(1)} %bitcast.43, bf16[4,2,3,128,1024]{4,3,2,1,0:T(8,128)(2,1)} %bitcast.48, bf16[4,3,9,2,1024]{4,3,2,1,0:T(2,128)(2,1)S(1)} %bitcast.45, f32[4,36,1024]{2,1,0:T(8,128)S(1)} %copy.11.refs_3_), custom_call_target="tpu_custom_call" | custom-call | flops 6442450944 | bytes 12582912 | tf_op jit(solution)/shard_map/shift_elementals/pallas_call | solution.py:168
  89.8 9.4 %halo_elementals.2 = bf16[1,8,128,128]{3,2,1,0:T(8,128)(2,1)S(1)} custom-call(s32[2,1]{1,0:T(2,128)S(1)} %get-tuple-element.17.refs_0_, bf16[4,2,3,128,1024]{4,3,2,1,0:T(8,128)(2,1)} %bitcast.49, bf16[4,3,9,2,1024]{4,3,2,1,0:T(2,128)(2,1)S(1)} %bitcast.46, f32[4,36,1024]{2,1,0:T(8,128)S(1)} %copy.11.refs_3_, ...), custom_call_target="tpu_custom_call" | custom-call | flops 3221225472 | bytes 6291456 | tf_op jit(solution)/shard_map/halo_elementals/pallas_call | solution.py:168
  99.2 1.1 copy_bitcast_fusion
  100.3 6.0 %all-to-all-start = ((bf16[16,3,8,8,128]{4,3,2,1,0:T(8,128)(2,1)}), bf16[16,3,8,8,128]{4,3,2,1,0:T(8,128)(2,1)S(1)}, u32[]{:S(2)}, u32[]{:S(2)}) async-start(bf16[16,3,8,8,128]{4,3,2,1,0:T(8,128)(2,1)} %copy_bitcast_fusion), calls=%async_computation | async-start | bytes 1572864 | tf_op jit(solution)/shard_map/all_to_all | solution.py:225
  106.3 0.7 sort.35
  107.1 17.8 %all-to-all-done = bf16[16,3,8,8,128]{4,3,2,1,0:T(8,128)(2,1)S(1)} async-done(((bf16[16,3,8,8,128]{4,3,2,1,0:T(8,128)(2,1)}), bf16[16,3,8,8,128]{4,3,2,1,0:T(8,128)(2,1)S(1)}, u32[]{:S(2)}, u32[]{:S(2)}) %all-to-all-start) | async-done | bytes 786464 | tf_op jit(solution)/shard_map/all_to_all | solution.py:225
  125.1 0.6 gather_fusion.1
  125.7 0.7 broadcast_select_fusion
  (31 shorter events, 1.9 us)
Async XLA Ops:
  6.1 13.2 %copy-start.2 = (s32[4]{0:T(128)S(1)}, s32[4]{0:T(128)}, u32[]{:S(2)}) copy-start(s32[4]{0:T(128)} %param.9) | copy-start | bytes 52
  6.1 19.1 %copy-start.3 = (s32[3]{0:T(128)S(1)}, s32[3]{0:T(128)}, u32[]{:S(2)}) copy-start(s32[3]{0:T(128)} %param.7) | copy-start | bytes 40
  13.2 76.6 %collective-permute-start = (bf16[2,3,128,1024]{3,2,1,0:T(8,128)(2,1)}, bf16[2,3,128,1024]{3,2,1,0:T(8,128)(2,1)S(1)}, u32[]{:S(2)}, u32[]{:S(2)}) collective-permute-start(bf16[2,3,128,1024]{3,2,1,0:T(8,128)(2,1)} %get-tuple-element.11), channel_id=1, source_target_pairs={{0,15},{1,0},{2,1},{3,2},{4,3},{5,4},{6,5},{7,6},{8,7},{9,8},{10,9... | collective-permute-start | bytes 4718600 | tf_op jit(solution)/shard_map/ppermute | solution.py:205
  18.6 35.1 %collective-permute-start.1 = (bf16[2,3,128,1024]{3,2,1,0:T(8,128)(2,1)}, bf16[2,3,128,1024]{3,2,1,0:T(8,128)(2,1)}, u32[]{:S(2)}, u32[]{:S(2)}) collective-permute-start(bf16[2,3,128,1024]{3,2,1,0:T(8,128)(2,1)} %get-tuple-element.16), channel_id=1, source_target_pairs={{0,15},{1,0},{2,1},{3,2},{4,3},{5,4},{6,5},{7,6},{8,7},{9,8},{10,9... | collective-permute-start | bytes 4718600 | tf_op jit(solution)/shard_map/ppermute | solution.py:205
  33.2 1.0 copy-start.1
  33.3 20.4 %copy-start = (bf16[4,3,2,3,3,1,1024]{6,2,5,4,3,1,0:T(2,128)(2,1)S(1)}, bf16[4,3,2,3,3,1,1024]{6,2,5,4,3,1,0:T(2,128)(2,1)}, u32[]{:S(2)}) copy-start(bf16[4,3,2,3,3,1,1024]{6,2,5,4,3,1,0:T(2,128)(2,1)} %param.6) | copy-start | bytes 1327108
  64.4 35.9 %all-to-all-start.1 = ((bf16[16,1,8,8,128]{4,3,2,1,0:T(8,128)(2,1)}), bf16[16,1,8,8,128]{4,3,2,1,0:T(8,128)(2,1)S(1)}, u32[]{:S(2)}, u32[]{:S(2)}) async-start(bf16[16,1,8,8,128]{4,3,2,1,0:T(8,128)(2,1)} %copy_bitcast_fusion.1), calls=%async_computation.1 | async-start | bytes 524288 | tf_op jit(solution)/shard_map/all_to_all | solution.py:225
  100.3 24.7 %all-to-all-start = ((bf16[16,3,8,8,128]{4,3,2,1,0:T(8,128)(2,1)}), bf16[16,3,8,8,128]{4,3,2,1,0:T(8,128)(2,1)S(1)}, u32[]{:S(2)}, u32[]{:S(2)}) async-start(bf16[16,3,8,8,128]{4,3,2,1,0:T(8,128)(2,1)} %copy_bitcast_fusion), calls=%async_computation | async-start | bytes 1572864 | tf_op jit(solution)/shard_map/all_to_all | solution.py:225
where the time goes:
time: 127 us; the launch traced here: 126 us
  Pallas kernels  38.7 us (30%)
  waiting for transfers between devices  36.7 us (29%)
  starting transfers between devices  18.1 us (14%)
  local copies, waits for them, and re-layouts  14 us (11%)
  between operations  12.8 us (10%)
  other arithmetic  6.12 us (5%)
    pallas_call x3, Pallas kernels, elementals_call(): pl.pallas_call(body, out_shape=jax.ShapeDtypeStruct((count, 2 * BLK, nev,...  38.7 us
    ppermute x2, waiting for transfers between devices, on_device(): lax.ppermute(lax.dynamic_index_in_dim(vectors, order[half + n], 0, keepdi...  18.9 us
    all_to_all x2, waiting for transfers between devices, spread(): parts = lax.all_to_all(parts, 'space', 0, 0, tiled=True)  17.8 us
    all_to_all x2, starting transfers between devices, spread(): parts = lax.all_to_all(parts, 'space', 0, 0, tiled=True)  12 us
    squeeze x1, local copies, waits for them, and re-layouts, on_device(): lax.dynamic_index_in_dim(vectors, order[half + n], 0, keepdims=False)  7.05 us
    ppermute x2, starting transfers between devices, on_device(): lax.ppermute(lax.dynamic_index_in_dim(vectors, order[half + n], 0, keepdi...  6.15 us
  transfers between devices with their start and end apart: 4, of which 2 were waited for; matrix products, arithmetic and copies ran while one was open for 8% of the time, Pallas kernels for 31%

commit v1 on v0

v1 whole, which is shorter than its diff:
```python
import functools
import math

import jax
import jax.numpy as jnp
from jax import lax
from jax.experimental import pallas as pl
from jax.experimental.pallas import tpu as pltpu
from jax.sharding import PartitionSpec as P

BLK = 4
LY = 32
LZ = 32
SUB = 8
LANES = 128
MIB = 1024 * 1024

epsilon_cycles = ((0, 1, 2), (1, 2, 0), (2, 0, 1))


def nth_slice(dir_ref, tsl, zero, last):
    index = jnp.int32(0)
    for t in range(tsl) if last else reversed(range(tsl)):
        index = jnp.where((dir_ref[t] == 0) == zero, jnp.int32(t), index)
    return index


def floor_mod(value, extent):
    if extent & (extent - 1) == 0:
        return value & (extent - 1)
    return jnp.remainder(value, extent)


def copy_kernel(dir_ref, in_ref, out_ref):
    out_ref[...] = in_ref[0]


def plane_to_send(directions, vectors, last):
    tsl, _, _, nev, sites = vectors.shape
    return pl.pallas_call(
        copy_kernel,
        out_shape=jax.ShapeDtypeStruct((2, 3, nev, sites), vectors.dtype),
        grid_spec=pltpu.PrefetchScalarGridSpec(
            num_scalar_prefetch=1,
            grid=(2, 3),
            in_specs=[
                pl.BlockSpec(
                    (1, 1, 1, nev, sites),
                    lambda r, k, d: (nth_slice(d, tsl, True, last), r, k, 0, 0),
                )
            ],
            out_specs=pl.BlockSpec((1, 1, nev, sites), lambda r, k, d: (r, k, 0, 0)),
        ),
        name="plane_to_send",
    )(directions, vectors)


def shift_inside(direction, vec_ref, src_ref):
    nev, sites = vec_ref.shape[-2:]
    rows_step = 2 * SUB

    def fill(shifted):
        def step(block, carry):
            rows = pl.ds(pl.multiple_of(block * rows_step, rows_step), rows_step)
            for part in range(2):
                for color in range(3):
                    values = vec_ref[0, part, color, rows, :].astype(jnp.float32)
                    src_ref[part, color, rows, :] = shifted(values).astype(jnp.bfloat16)
            return carry

        lax.fori_loop(0, nev // rows_step, step, 0)

    def along_third(values):
        lane = lax.broadcasted_iota(jnp.int32, values.shape, 1)
        ahead = pltpu.roll(values, sites - 1, 1)
        wrapped = pltpu.roll(values, LZ - 1, 1)
        return jnp.where(lane % LZ == LZ - 1, wrapped, ahead)

    @pl.when(direction == 1)
    def _():
        fill(lambda values: pltpu.roll(values, sites - LZ, 1))

    @pl.when(direction != 1)
    def _():
        fill(along_third)


def phase_rows(mom_ref, extent, sites):
    shape = (SUB, sites)
    site = lax.broadcasted_iota(jnp.int32, shape, 1)
    x_site = lax.axis_index("space")
    x_part = floor_mod(jnp.full(shape, mom_ref[0] * x_site, jnp.int32), extent)
    y_part = floor_mod(mom_ref[1] * (site // LZ), LY)
    z_part = floor_mod(mom_ref[2] * (site % LZ), LZ)
    turns = (
        x_part.astype(jnp.float32) / extent
        + y_part.astype(jnp.float32) / LY
        + z_part.astype(jnp.float32) / LZ
    )
    angles = -2.0 * math.pi * turns
    return jnp.cos(angles), jnp.sin(angles)


def elementals_kernel(shifting, extent, scale, tsl, *refs):
    dir_ref, off_ref, mom_ref, vec_ref, link_ref = refs[:5]
    if shifting:
        out_ref, prod_ref, rhs_ref, acc_ref, u_ref, lead_ref, src_ref = refs[5:]
        which = pl.program_id(0)
        t = jnp.where(
            which == 0, nth_slice(dir_ref, tsl, False, False), nth_slice(dir_ref, tsl, False, True)
        )
        shift_inside(dir_ref[t], vec_ref, src_ref)
    else:
        src_ref, _, out_ref, prod_ref, rhs_ref, acc_ref, u_ref, lead_ref = refs[5:]
        t = nth_slice(dir_ref, tsl, True, shifting is None)
    nev, sites = vec_ref.shape[-2:]
    half = nev // 2
    blocks = sites // LANES

    for entry in range(9):
        pair = link_ref[0, 0, entry].astype(jnp.float32)
        u_re, u_im = pair[0:1], pair[1:2]
        u_ref[entry : entry + 1, :] = u_re
        u_ref[9 + entry : 10 + entry, :] = u_im - u_re
        u_ref[18 + entry : 19 + entry, :] = u_re + u_im

    cosine, sine = phase_rows(mom_ref, extent, sites)
    row_id = lax.broadcasted_iota(jnp.int32, (SUB, nev), 0)
    col_id = lax.broadcasted_iota(jnp.int32, (SUB, nev), 1)
    chosen = jnp.where(col_id == row_id + off_ref[t], 1.0, 0.0).astype(jnp.bfloat16)
    for color in range(3):
        raw_re = jnp.dot(chosen, vec_ref[0, 0, color], preferred_element_type=jnp.float32)
        raw_im = jnp.dot(chosen, vec_ref[0, 1, color], preferred_element_type=jnp.float32)
        lead_re = raw_re * cosine - raw_im * sine
        lead_im = raw_re * sine + raw_im * cosine
        lead_ref[color * SUB : (color + 1) * SUB, :] = lead_re
        lead_ref[(3 + color) * SUB : (4 + color) * SUB, :] = lead_im - lead_re
        lead_ref[(6 + color) * SUB : (7 + color) * SUB, :] = lead_re + lead_im

    for color in range(3):
        for block in range(blocks):
            lanes = slice(block * LANES, (block + 1) * LANES)
            vec_re = vec_ref[0, 0, color, :, lanes]
            vec_im = vec_ref[0, 1, color, :, lanes]
            first = slice(2 * color * LANES, (2 * color + 1) * LANES)
            second = slice((2 * color + 1) * LANES, (2 * color + 2) * LANES)
            rhs_ref[block, 0:nev, first] = vec_re
            rhs_ref[block, nev : 2 * nev, first] = vec_im
            rhs_ref[block, 0:nev, second] = -vec_im
            rhs_ref[block, nev : 2 * nev, second] = vec_re

    acc_ref[...] = jnp.zeros_like(acc_ref)
    prod_ref[1] = jnp.zeros_like(prod_ref[1])

    def vector_part(lane, which):
        lanes = pl.ds(lane, LANES)

        def row(ref, index):
            return jnp.broadcast_to(ref[pl.ds(index, 1), lanes], (SUB, LANES))

        for block in range(half // SUB):
            rows = slice(which * half + block * SUB, which * half + (block + 1) * SUB)
            s_re = [src_ref[0, j, rows, lanes].astype(jnp.float32) for j in range(3)]
            s_im = [src_ref[1, j, rows, lanes].astype(jnp.float32) for j in range(3)]
            s_sum = [s_re[j] + s_im[j] for j in range(3)]
            d_re, d_im, d_sum = [], [], []
            for i in range(3):
                k1 = k2 = k3 = None
                for j in range(3):
                    entry = 3 * i + j
                    t1 = row(u_ref, entry) * s_sum[j]
                    t2 = row(u_ref, 9 + entry) * s_re[j]
                    t3 = row(u_ref, 18 + entry) * s_im[j]
                    k1 = t1 if k1 is None else k1 + t1
                    k2 = t2 if k2 is None else k2 + t2
                    k3 = t3 if k3 is None else k3 + t3
                re = (k1 - k3).astype(jnp.bfloat16).astype(jnp.float32)
                im = (k1 + k2).astype(jnp.bfloat16).astype(jnp.float32)
                d_re.append(re)
                d_im.append(im)
                d_sum.append(re + im)
            for a in range(BLK):
                out_rows = slice(a * half + block * SUB, a * half + (block + 1) * SUB)
                for i, j, k in epsilon_cycles:
                    at_i, at_j = i * SUB + a, j * SUB + a
                    k1 = row(lead_ref, at_i) * d_sum[j] - row(lead_ref, at_j) * d_sum[i]
                    at_i, at_j = at_i + 3 * SUB, at_j + 3 * SUB
                    k2 = row(lead_ref, at_i) * d_re[j] - row(lead_ref, at_j) * d_re[i]
                    at_i, at_j = at_i + 3 * SUB, at_j + 3 * SUB
                    k3 = row(lead_ref, at_i) * d_im[j] - row(lead_ref, at_j) * d_im[i]
                    first = slice(2 * k * LANES, (2 * k + 1) * LANES)
                    second = slice((2 * k + 1) * LANES, (2 * k + 2) * LANES)
                    prod_ref[which, out_rows, first] = (k1 - k3).astype(jnp.bfloat16)
                    prod_ref[which, out_rows, second] = (k1 + k2).astype(jnp.bfloat16)

    def matrix_part(block, which):
        acc_ref[which] += lax.dot_general(
            prod_ref[which],
            rhs_ref[block],
            (((1,), (1,)), ((), ())),
            preferred_element_type=jnp.float32,
        )

    def lane_step(block, carry):
        lane = pl.multiple_of(block * LANES, LANES)
        matrix_part(jnp.maximum(block - 1, 0), 1)
        vector_part(lane, 0)
        matrix_part(block, 0)
        vector_part(lane, 1)
        return carry

    lax.fori_loop(0, blocks, lane_step, 0)
    matrix_part(blocks - 1, 1)

    for which in range(2):
        for a in range(BLK):
            for part in range(2):
                block = acc_ref[
                    which, a * half : (a + 1) * half, part * nev : (part + 1) * nev
                ]
                block = (block * scale).astype(jnp.bfloat16)
                where = part * BLK + a
                if len(out_ref.shape) == 5:
                    count = half // SUB
                    out_ref[which * count : (which + 1) * count, 0, where] = block.reshape(
                        count, SUB, nev
                    )
                else:
                    out_ref[0, where, which * half : (which + 1) * half] = block


def elementals_call(kind, place, total, extent, scale, scalars, vectors, links, source, into, tiled):
    shifting = kind == "inside"
    last = kind == "last"
    tsl, _, _, nev, sites = vectors.shape
    count = 2 if shifting else 1

    def index_of(n, d):
        if shifting:
            first = nth_slice(d, tsl, False, False)
            return jnp.where(n == 0, first, nth_slice(d, tsl, False, True))
        return nth_slice(d, tsl, True, last)

    in_specs = [
        pl.BlockSpec((1, 2, 3, nev, sites), lambda n, d, o, m: (index_of(n, d), 0, 0, 0, 0)),
        pl.BlockSpec(
            (1, 1, 9, 2, sites), lambda n, d, o, m: (index_of(n, d), d[index_of(n, d)], 0, 0, 0)
        ),
    ]
    operands = [*scalars, vectors, links]
    scratch = [
        pltpu.VMEM((2, BLK * nev // 2, 6 * LANES), jnp.bfloat16),
        pltpu.VMEM((sites // LANES, 2 * nev, 6 * LANES), jnp.bfloat16),
        pltpu.VMEM((2, BLK * nev // 2, 2 * nev), jnp.float32),
        pltpu.VMEM((32, sites), jnp.float32),
        pltpu.VMEM((9 * SUB, sites), jnp.float32),
    ]
    aliases = {}
    if shifting:
        scratch.append(pltpu.VMEM((2, 3, nev, sites), jnp.bfloat16))
    else:
        in_specs.append(pl.BlockSpec((2, 3, nev, sites), lambda n, d, o, m: (0, 0, 0, 0)))
        in_specs.append(pl.BlockSpec(memory_space=pl.ANY))
        operands += [source, into]
        if total > 1:
            aliases = {len(operands) - 1: 0}
    if tiled:
        shape = (nev // SUB, total, 2 * BLK, SUB, nev)
        block = (nev // SUB, 1, 2 * BLK, SUB, nev)
        out_spec = pl.BlockSpec(block, lambda n, d, o, m: (0, place + n, 0, 0, 0))
    else:
        shape = (total, 2 * BLK, nev, nev)
        block = (1, 2 * BLK, nev, nev)
        out_spec = pl.BlockSpec(block, lambda n, d, o, m: (place + n, 0, 0, 0))

    mode = True if shifting else (None if last else False)
    return pl.pallas_call(
        functools.partial(elementals_kernel, mode, extent, scale, tsl),
        out_shape=jax.ShapeDtypeStruct(shape, jnp.bfloat16),
        grid_spec=pltpu.PrefetchScalarGridSpec(
            num_scalar_prefetch=3,
            grid=(count,),
            in_specs=in_specs,
            out_specs=out_spec,
            scratch_shapes=scratch,
        ),
        input_output_aliases=aliases,
        compiler_params=pltpu.CompilerParams(
            dimension_semantics=("arbitrary",), vmem_limit_bytes=40 * MIB
        ),
        cost_estimate=pl.CostEstimate(
            flops=count * 16 * BLK * 3 * nev * nev * sites,
            bytes_accessed=count * 16 * 3 * nev * sites,
            transcendentals=0,
        ),
        name=kind + "_elementals",
    )(*operands)


def sum_kernel(first, *refs):
    in_ref, out_ref = refs[1], refs[-1]
    total = in_ref[0, 0].astype(jnp.float32)
    for device in range(1, in_ref.shape[0]):
        total = total + in_ref[device, 0].astype(jnp.float32)
    out_ref[0] = total


def sum_parts(directions, parts, first, tsl, into):
    devices, count = parts.shape[:2]
    body = parts.shape[2:]
    zeros = (0,) * len(body)

    def index_of(n, d):
        if not first:
            return nth_slice(d, tsl, True, True)
        one = nth_slice(d, tsl, False, False)
        two = nth_slice(d, tsl, False, True)
        return jnp.where(n == 0, one, jnp.where(n == 1, two, nth_slice(d, tsl, True, False)))

    in_specs = [pl.BlockSpec((devices, 1) + body, lambda n, d: (0, n) + zeros)]
    operands = [directions, parts]
    if not first:
        in_specs.append(pl.BlockSpec(memory_space=pl.ANY))
        operands.append(into)
    return pl.pallas_call(
        functools.partial(sum_kernel, first),
        out_shape=jax.ShapeDtypeStruct((tsl,) + body, jnp.float32),
        grid_spec=pltpu.PrefetchScalarGridSpec(
            num_scalar_prefetch=1,
            grid=(count,),
            in_specs=in_specs,
            out_specs=pl.BlockSpec((1,) + body, lambda n, d: (index_of(n, d),) + zeros),
        ),
        input_output_aliases={} if first else {2: 0},
        name="sum_parts",
    )(*operands)


def on_device(eigenvectors, link_field, momentum, directions, offsets):
    devices = lax.axis_size("space")
    tsl, _, _, nev, planes, sites = eigenvectors.shape
    assert planes == 1 and tsl == 4
    extent = planes * devices
    scale = 1.0 / math.sqrt(extent * sites)
    vectors = eigenvectors.reshape(tsl, 2, 3, nev, sites)
    links = jnp.transpose(link_field, (0, 1, 3, 4, 5, 2, 6)).reshape(tsl, 3, 9, 2, sites)
    tiled = nev // devices == SUB

    pairs = [(device, (device - 1) % devices) for device in range(devices)]
    halos = [
        lax.ppermute(plane_to_send(directions, vectors, last), "space", pairs)
        for last in (False, True)
    ]

    scalars = (directions, offsets, momentum)
    call = functools.partial(
        elementals_call,
        extent=extent,
        scale=scale,
        scalars=scalars,
        vectors=vectors,
        links=links,
        tiled=tiled,
    )
    early = call("inside", 0, 3, source=None, into=None)
    early = call("first", 2, 3, source=halos[0], into=early)
    late = call("last", 0, 1, source=halos[1], into=early)

    def exchange(partial):
        if not tiled:
            count = partial.shape[0]
            partial = partial.reshape(count, 2 * BLK, devices, nev // devices, nev)
            partial = jnp.moveaxis(partial, 2, 0)
        return lax.all_to_all(partial, "space", 0, 0, tiled=True)

    sums = sum_parts(directions, exchange(early), True, tsl, None)
    sums = sum_parts(directions, exchange(late), False, tsl, sums)
    return sums.reshape(tsl, 2, BLK, nev // devices, nev)


def solution(mesh):
    placed = (
        P("cfg", None, None, None, "space", None),
        P("cfg", None, None, None, None, "space", None),
        P(),
        P(),
        P(),
    )
    return jax.shard_map(
        on_device,
        mesh=mesh,
        in_specs=placed,
        out_specs=P("cfg", None, None, "space", None),
        check_vma=False,
    )
```

time: 127 us -> 85.5 us (0.67)
  waiting for transfers between devices: 36.7 us -> 15.1 us
  between operations: 12.8 us -> 0.07 us
  Pallas kernels: 38.7 us -> 47.1 us
  local copies, waits for them, and re-layouts: 14 us -> 7.3 us
  other arithmetic: 6.12 us -> 0 us
  starting transfers between devices: 18.1 us -> 15.3 us
    ppermute x2, waiting for transfers between devices: 18.9 us -> 0.01 us  [on_device(): lax.ppermute(plane_to_send(directions, vectors, last), 'space', pairs)]
    pallas_call x3 -> x7, Pallas kernels: 38.7 us -> 47.1 us  [the longest x3 31 us: elementals_call(): pl.pallas_call(functools.partial(elementals_kernel, mode, extent, scale,...]
    unnamed x8 -> x18, local copies, waits for them, and re-layouts: 0.03 us -> 7.3 us
    squeeze x1 -> x0, local copies, waits for them, and re-layouts: 7.05 us -> none  [on_device(): lax.dynamic_index_in_dim(vectors, order[half + n], 0, keepdims=False)]
    all_to_all x2, starting transfers between devices: 12 us -> 9.08 us  [exchange(): return lax.all_to_all(partial, 'space', 0, 0, tiled=True)]
    all_to_all x2, waiting for transfers between devices: 17.8 us -> 15.1 us  [exchange(): return lax.all_to_all(partial, 'space', 0, 0, tiled=True)]
    another operation x3 -> x0, local copies, waits for them, and re-layouts: 2.46 us -> none  [the longest x2 2.07 us: on_device(): jnp.stack([lax.dynamic_slice_in_dim(vectors[t], offsets[t], BLK, axis=2)...]
    slice x4 -> x0, local copies, waits for them, and re-layouts: 2.04 us -> none  [the longest x1 0.67 us: on_device(): order[half + n]]
  transfers between devices with their start and end apart: 4 -> 4, of which waited for: 2 -> 2; matrix products, arithmetic and copies ran while one was open for 8% -> 0% of each run, Pallas kernels for 31% -> 47%
where the time goes in v1:
time: 85.5 us; the launch traced here: 84.8 us
  Pallas kernels  47.1 us (55%)
  starting transfers between devices  15.3 us (18%)
  waiting for transfers between devices  15.1 us (18%)
  local copies, waits for them, and re-layouts  7.3 us (9%)
    pallas_call x3, Pallas kernels, elementals_call(): pl.pallas_call(functools.partial(elementals_kernel, mode, extent, scale,...  31 us
    all_to_all x2, waiting for transfers between devices, exchange(): return lax.all_to_all(partial, 'space', 0, 0, tiled=True)  15.1 us
    pallas_call x2, Pallas kernels, plane_to_send(): pl.pallas_call(copy_kernel, out_shape=jax.ShapeDtypeStruct((2, 3, nev, si...  10.5 us
    all_to_all x2, starting transfers between devices, exchange(): return lax.all_to_all(partial, 'space', 0, 0, tiled=True)  9.08 us
    unnamed x18, local copies, waits for them, and re-layouts  7.3 us
    ppermute x2, starting transfers between devices, on_device(): lax.ppermute(plane_to_send(directions, vectors, last), 'space', pairs)  6.2 us
    pallas_call x2, Pallas kernels, sum_parts(): pl.pallas_call(functools.partial(sum_kernel, first), out_shape=jax.ShapeD...  5.6 us
  transfers between devices with their start and end apart: 4, of which 2 were waited for; matrix products, arithmetic and copies ran while one was open for 0% of the time, Pallas kernels for 47%

profile of v1, /device:TPU:0, one launch (start us, length us, event | category | flops | bytes accessed | tf_op | source)
XLA Modules:
  0.0 84.8 jit_solution(7879413029224785798)
XLA Ops:
  0.0 5.2 %plane_to_send.3 = bf16[2,3,128,1024]{3,2,1,0:T(8,128)(2,1)} custom-call(s32[4]{0:T(128)} %refs_0_.9, bf16[4,2,3,128,1024]{4,3,2,1,0:T(8,128)(2,1)} %bitcast.5), custom_call_target="tpu_custom_call" | custom-call | tf_op jit(solution)/shard_map/plane_to_send/pallas_call | solution.py:40
  5.3 5.5 %collective-permute-start.1 = (bf16[2,3,128,1024]{3,2,1,0:T(8,128)(2,1)}, bf16[2,3,128,1024]{3,2,1,0:T(8,128)(2,1)S(1)}, u32[]{:S(2)}, u32[]{:S(2)}) collective-permute-start(bf16[2,3,128,1024]{3,2,1,0:T(8,128)(2,1)} %plane_to_send.3), channel_id=1, source_target_pairs={{0,15},{1,0},{2,1},{3,2},{4,3},{5,4},{6,5},{7,6},{8,7},{9,8},{10,9... | collective-permute-start | bytes 4718600 | tf_op jit(solution)/shard_map/ppermute | solution.py:351
  10.8 5.2 %plane_to_send.2 = bf16[2,3,128,1024]{3,2,1,0:T(8,128)(2,1)} custom-call(s32[4]{0:T(128)} %refs_0_.9, bf16[4,2,3,128,1024]{4,3,2,1,0:T(8,128)(2,1)} %bitcast.6), custom_call_target="tpu_custom_call" | custom-call | tf_op jit(solution)/shard_map/plane_to_send/pallas_call | solution.py:40
  16.0 0.7 collective-permute-start
  16.7 0.0 copy-done.2
  16.7 0.0 copy-done.5
  16.7 2.8 %copy-done = bf16[4,2,3,128,1,1024]{5,3,4,2,1,0:T(8,128)(2,1)S(1)} copy-done((bf16[4,2,3,128,1,1024]{5,3,4,2,1,0:T(8,128)(2,1)S(1)}, bf16[4,2,3,128,1,1024]{5,3,4,2,1,0:T(8,128)(2,1)}, u32[]{:S(2)}) %copy-start) | copy-done | bytes 6291480
  19.5 1.0 %copy-done.3 = bf16[4,3,2,3,3,1,1024]{6,2,5,4,3,1,0:T(2,128)(2,1)S(1)} copy-done((bf16[4,3,2,3,3,1,1024]{6,2,5,4,3,1,0:T(2,128)(2,1)S(1)}, bf16[4,3,2,3,3,1,1024]{6,2,5,4,3,1,0:T(2,128)(2,1)}, u32[]{:S(2)}) %copy-start.3) | copy-done | bytes 442392
  20.5 16.1 %inside_elementals.1.refs_6_ = bf16[16,3,8,8,128]{4,3,2,1,0:T(8,128)(2,1)} custom-call(s32[4]{0:T(128)S(1)} %copy-done.2, s32[4]{0:T(128)S(1)} %copy-done.5, s32[3]{0:T(128)S(1)} %copy-done.6, bf16[4,2,3,128,1024]{4,3,2,1,0:T(8,128)(2,1)S(1)} %bitcast.7, bf16[4,3,9,2,1024]{4,3,2,1,0:T(2,128)(2,1)S(1)} %bitcast.10), custom_call_target="tpu_custom_call" | custom-call | flops 6442450944 | bytes 12582912 | tf_op jit(solution)/shard_map/inside_elementals/pallas_call | solution.py:277
  36.6 0.0 collective-permute-done.1.refs_5_
  36.6 7.5 %first_elementals.1.refs_6_ = bf16[16,3,8,8,128]{4,3,2,1,0:T(8,128)(2,1)} custom-call(s32[4]{0:T(128)S(1)} %copy-done.2, s32[4]{0:T(128)S(1)} %copy-done.5, s32[3]{0:T(128)S(1)} %copy-done.6, bf16[4,2,3,128,1024]{4,3,2,1,0:T(8,128)(2,1)S(1)} %bitcast.8, bf16[4,3,9,2,1024]{4,3,2,1,0:T(2,128)(2,1)S(1)} %bitcast.11, ...), custom_call_target="tpu_custom_call", output_to_operand_aliasing={{}: (6, {})} | custom-call | flops 3221225472 | bytes 6291456 | tf_op jit(solution)/shard_map/first_elementals/pallas_call | solution.py:277
  44.1 3.7 %all-to-all-start.1 = ((bf16[16,3,8,8,128]{4,3,2,1,0:T(8,128)(2,1)}), bf16[16,3,8,8,128]{4,3,2,1,0:T(8,128)(2,1)S(1)}, u32[]{:S(2)}, u32[]{:S(2)}) async-start(bf16[16,3,8,8,128]{4,3,2,1,0:T(8,128)(2,1)} %first_elementals.1.refs_6_), calls=%async_computation.1 | async-start | bytes 1572864 | tf_op jit(solution)/shard_map/all_to_all | solution.py:374
  47.8 0.0 collective-permute-done.refs_5_
  47.8 0.0 copy-done.4
  47.8 0.0 copy-start.1
  47.8 2.8 %copy-done.1 = bf16[4,2,3,128,1,1024]{5,3,4,2,1,0:T(8,128)(2,1)S(1)} copy-done((bf16[4,2,3,128,1,1024]{5,3,4,2,1,0:T(8,128)(2,1)S(1)}, bf16[4,2,3,128,1,1024]{5,3,4,2,1,0:T(8,128)(2,1)}, u32[]{:S(2)}) %copy-start.1) | copy-done | bytes 6291480
  50.6 7.4 %last_elementals.1 = bf16[16,1,8,8,128]{4,3,2,1,0:T(8,128)(2,1)} custom-call(s32[4]{0:T(128)S(1)} %copy-done.2, s32[4]{0:T(128)S(1)} %copy-done.5, s32[3]{0:T(128)S(1)} %copy-done.6, bf16[4,2,3,128,1024]{4,3,2,1,0:T(8,128)(2,1)S(1)} %bitcast.9, bf16[4,3,9,2,1024]{4,3,2,1,0:T(2,128)(2,1)S(1)} %bitcast.12, ...), custom_call_target="tpu_custom_call" | custom-call | flops 3221225472 | bytes 6291456 | tf_op jit(solution)/shard_map/last_elementals/pallas_call | solution.py:277
  58.1 8.4 %all-to-all-done.1.refs_1_ = bf16[16,3,8,8,128]{4,3,2,1,0:T(8,128)(2,1)S(1)} async-done(((bf16[16,3,8,8,128]{4,3,2,1,0:T(8,128)(2,1)}), bf16[16,3,8,8,128]{4,3,2,1,0:T(8,128)(2,1)S(1)}, u32[]{:S(2)}, u32[]{:S(2)}) %all-to-all-start.1) | async-done | bytes 786464 | tf_op jit(solution)/shard_map/all_to_all | solution.py:374
  66.5 5.3 %all-to-all-start = ((bf16[16,1,8,8,128]{4,3,2,1,0:T(8,128)(2,1)}), bf16[16,1,8,8,128]{4,3,2,1,0:T(8,128)(2,1)S(1)}, u32[]{:S(2)}, u32[]{:S(2)}) async-start(bf16[16,1,8,8,128]{4,3,2,1,0:T(8,128)(2,1)} %last_elementals.1), calls=%async_computation | async-start | bytes 524288 | tf_op jit(solution)/shard_map/all_to_all | solution.py:374
  71.8 0.0 copy-done.7
  71.8 3.3 %sum_parts.2.refs_2_ = f32[4,8,8,128]{3,2,1,0:T(8,128)} custom-call(s32[4]{0:T(128)} %refs_0_.9, bf16[16,3,8,8,128]{4,3,2,1,0:T(8,128)(2,1)} %copy-done.7), custom_call_target="tpu_custom_call" | custom-call | tf_op jit(solution)/shard_map/sum_parts/pallas_call | solution.py:325
  75.1 6.7 %all-to-all-done.refs_1_ = bf16[16,1,8,8,128]{4,3,2,1,0:T(8,128)(2,1)S(1)} async-done(((bf16[16,1,8,8,128]{4,3,2,1,0:T(8,128)(2,1)}), bf16[16,1,8,8,128]{4,3,2,1,0:T(8,128)(2,1)S(1)}, u32[]{:S(2)}, u32[]{:S(2)}) %all-to-all-start) | async-done | bytes 262176 | tf_op jit(solution)/shard_map/all_to_all | solution.py:374
  81.8 0.7 copy-done.8
  82.5 2.3 %sum_parts.3 = f32[4,8,8,128]{3,2,1,0:T(8,128)} custom-call(s32[4]{0:T(128)} %refs_0_.9, bf16[16,1,8,8,128]{4,3,2,1,0:T(8,128)(2,1)} %copy-done.8, f32[4,8,8,128]{3,2,1,0:T(8,128)} %sum_parts.2.refs_2_), custom_call_target="tpu_custom_call", output_to_operand_aliasing={{}: (2, {})} | custom-call | tf_op jit(solution)/shard_map/sum_parts/pallas_call | solution.py:325
  (9 shorter events, 0.0 us)
Async XLA Ops:
  5.2 11.5 %copy-start.2 = (s32[4]{0:T(128)S(1)}, s32[4]{0:T(128)}, u32[]{:S(2)}) copy-start(s32[4]{0:T(128)} %refs_0_.9) | copy-start | bytes 52
  5.3 11.5 %copy-start.5 = (s32[4]{0:T(128)S(1)}, s32[4]{0:T(128)}, u32[]{:S(2)}) copy-start(s32[4]{0:T(128)} %refs_1_.5) | copy-start | bytes 52
  5.3 11.5 %copy-start.6 = (s32[3]{0:T(128)S(1)}, s32[3]{0:T(128)}, u32[]{:S(2)}) copy-start(s32[3]{0:T(128)} %refs_2_.5) | copy-start | bytes 40
  5.3 31.4 %collective-permute-start.1 = (bf16[2,3,128,1024]{3,2,1,0:T(8,128)(2,1)}, bf16[2,3,128,1024]{3,2,1,0:T(8,128)(2,1)S(1)}, u32[]{:S(2)}, u32[]{:S(2)}) collective-permute-start(bf16[2,3,128,1024]{3,2,1,0:T(8,128)(2,1)} %plane_to_send.3), channel_id=1, source_target_pairs={{0,15},{1,0},{2,1},{3,2},{4,3},{5,4},{6,5},{7,6},{8,7},{9,8},{10,9... | collective-permute-start | bytes 4718600 | tf_op jit(solution)/shard_map/ppermute | solution.py:351
  16.0 31.8 %collective-permute-start = (bf16[2,3,128,1024]{3,2,1,0:T(8,128)(2,1)}, bf16[2,3,128,1024]{3,2,1,0:T(8,128)(2,1)S(1)}, u32[]{:S(2)}, u32[]{:S(2)}) collective-permute-start(bf16[2,3,128,1024]{3,2,1,0:T(8,128)(2,1)} %plane_to_send.2), channel_id=1, source_target_pairs={{0,15},{1,0},{2,1},{3,2},{4,3},{5,4},{6,5},{7,6},{8,7},{9,8},{10,9... | collective-permute-start | bytes 4718600 | tf_op jit(solution)/shard_map/ppermute | solution.py:351
  16.7 2.8 %copy-start = (bf16[4,2,3,128,1,1024]{5,3,4,2,1,0:T(8,128)(2,1)S(1)}, bf16[4,2,3,128,1,1024]{5,3,4,2,1,0:T(8,128)(2,1)}, u32[]{:S(2)}) copy-start(bf16[4,2,3,128,1,1024]{5,3,4,2,1,0:T(8,128)(2,1)} %param.5) | copy-start | bytes 18874372
  19.5 1.0 %copy-start.3 = (bf16[4,3,2,3,3,1,1024]{6,2,5,4,3,1,0:T(2,128)(2,1)S(1)}, bf16[4,3,2,3,3,1,1024]{6,2,5,4,3,1,0:T(2,128)(2,1)}, u32[]{:S(2)}) copy-start(bf16[4,3,2,3,3,1,1024]{6,2,5,4,3,1,0:T(2,128)(2,1)} %param.6) | copy-start | bytes 1327108
  44.1 3.8 %copy-start.4 = (bf16[4,3,2,3,3,1,1024]{6,2,5,4,3,1,0:T(2,128)(2,1)S(1)}, bf16[4,3,2,3,3,1,1024]{6,2,5,4,3,1,0:T(2,128)(2,1)}, u32[]{:S(2)}) copy-start(bf16[4,3,2,3,3,1,1024]{6,2,5,4,3,1,0:T(2,128)(2,1)} %param.6) | copy-start | bytes 1327108
  44.1 22.4 %all-to-all-start.1 = ((bf16[16,3,8,8,128]{4,3,2,1,0:T(8,128)(2,1)}), bf16[16,3,8,8,128]{4,3,2,1,0:T(8,128)(2,1)S(1)}, u32[]{:S(2)}, u32[]{:S(2)}) async-start(bf16[16,3,8,8,128]{4,3,2,1,0:T(8,128)(2,1)} %first_elementals.1.refs_6_), calls=%async_computation.1 | async-start | bytes 1572864 | tf_op jit(solution)/shard_map/all_to_all | solution.py:374
  47.8 2.8 %copy-start.1 = (bf16[4,2,3,128,1,1024]{5,3,4,2,1,0:T(8,128)(2,1)S(1)}, bf16[4,2,3,128,1,1024]{5,3,4,2,1,0:T(8,128)(2,1)}, u32[]{:S(2)}) copy-start(bf16[4,2,3,128,1,1024]{5,3,4,2,1,0:T(8,128)(2,1)} %param.5) | copy-start | bytes 18874372
  66.5 5.3 %copy-start.7 = (bf16[16,3,8,8,128]{4,3,2,1,0:T(8,128)(2,1)}, bf16[16,3,8,8,128]{4,3,2,1,0:T(8,128)(2,1)S(1)}, u32[]{:S(2)}) copy-start(bf16[16,3,8,8,128]{4,3,2,1,0:T(8,128)(2,1)S(1)} %all-to-all-done.1.refs_1_) | copy-start | bytes 2359300
  66.5 15.4 %all-to-all-start = ((bf16[16,1,8,8,128]{4,3,2,1,0:T(8,128)(2,1)}), bf16[16,1,8,8,128]{4,3,2,1,0:T(8,128)(2,1)S(1)}, u32[]{:S(2)}, u32[]{:S(2)}) async-start(bf16[16,1,8,8,128]{4,3,2,1,0:T(8,128)(2,1)} %last_elementals.1), calls=%async_computation | async-start | bytes 524288 | tf_op jit(solution)/shard_map/all_to_all | solution.py:374
  81.8 0.7 copy-start.8
